TPU v7x, 32 devices: a whole 2x2x4 slice. The times are simulated.
32 devices in a mesh: virt: 2 (over y), occ: 4 (over z), aux: 4 (over x, core).
Axes of the slice: x: 2, y: 2, z: 4, core: 2. Of those that a mesh axis runs over, the one named last changes fastest.
Arguments:
- three_index: bfloat16 [16384, 4, 1536], P('aux', 'occ', 'virt'), may hold values from -0.59765625 to 0.59765625
- occupied_energy: bfloat16 [4], P('occ'), may hold values from -2 to -0.5
- virtual_energy: float32 [1536], P('virt'), may hold values from 0.2 to 3
Outputs:
- density: bfloat16 [16384, 4, 1536], P('aux', 'occ', 'virt')
All inputs are finite; a program needn't handle non-finite values.
Results may differ from a plain program's by a relative error of at most 0.0046.
Values may be sent and summed in bfloat16 or wider, within the bound.
A program may use at most 128 MiB of HBM per device.

v0:
```python
import jax
import jax.numpy as jnp
from jax import lax
from jax.sharding import PartitionSpec as P

spin_scale = 1.2


def shifted(block, axis, distance):
    devices = range(lax.axis_size(axis))
    route = [((i - distance) % len(devices), i) for i in devices]
    return lax.ppermute(block, axis, route)


def level_matrix(virtual_energy, left_occupied, right_occupied):
    left_levels = (virtual_energy[None, :] - left_occupied.astype(jnp.float32)[:, None]).reshape(-1)
    right_levels = (virtual_energy[None, :] - right_occupied.astype(jnp.float32)[:, None]).reshape(
        -1
    )
    return left_levels[:, None] + right_levels[None, :]


def amplitudes(own_block, far_block, own_energy, far_energy, virtual_energy):
    partial_sums = lax.dot_general(
        own_block, far_block, (((0,), (0,)), ((), ())), preferred_element_type=jnp.float32
    )
    pair_sums = lax.psum(partial_sums, "aux")
    denominator = level_matrix(virtual_energy, own_energy, far_energy)
    return (spin_scale * pair_sums / denominator).astype(jnp.bfloat16)


def on_device(three_index, occupied_energy, virtual_energy):
    aux_rows, occ_rows, slab_size = three_index.shape
    own_block = three_index.reshape(aux_rows, occ_rows * slab_size)
    first_index, first_energy = shifted((three_index, occupied_energy), "occ", 1)
    second_index, second_energy = shifted((first_index, first_energy), "occ", 1)
    first_block = first_index.reshape(aux_rows, occ_rows * slab_size)
    second_block = second_index.reshape(aux_rows, occ_rows * slab_size)
    later_one = shifted(own_block, "occ", -1)
    later_two = shifted(own_block, "occ", -2)
    first_amplitude = amplitudes(
        own_block, first_block, occupied_energy, first_energy, virtual_energy
    )
    accumulated = lax.dot_general(
        first_block, first_amplitude, (((1,), (1,)), ((), ())), preferred_element_type=jnp.float32
    )
    arrived_one = shifted(first_amplitude, "occ", -1)
    accumulated = accumulated + jnp.dot(later_one, arrived_one, preferred_element_type=jnp.float32)
    second_amplitude = amplitudes(
        own_block, second_block, occupied_energy, second_energy, virtual_energy
    )
    accumulated = accumulated + lax.dot_general(
        second_block, second_amplitude, (((1,), (1,)), ((), ())), preferred_element_type=jnp.float32
    )
    arrived_two = shifted(second_amplitude, "occ", -2)
    accumulated = accumulated + jnp.dot(later_two, arrived_two, preferred_element_type=jnp.float32)
    return accumulated.astype(jnp.bfloat16).reshape(aux_rows, occ_rows, slab_size)


def solution(mesh):
    placed = (P("aux", "occ", "virt"), P("occ"), P("virt"))
    return jax.shard_map(
        on_device, mesh=mesh, in_specs=placed, out_specs=P("aux", "occ", "virt"), check_vma=False
    )
```

profile of v0, /device:TPU:0, one launch (start us, length us, event | category | flops | bytes accessed | tf_op | source)
XLA Modules:
  0.0 827.2 jit_solution(13724107224548925239)
XLA Ops:
  6.5 0.0 all-reduce.3.cloned.1.call-start
  6.5 3.1 collective-permute-start
  9.6 137.7 %collective-permute-done = bf16[4096,1,768]{2,0,1:T(8,128)(2,1)S(1)} collective-permute-done((bf16[4096,1,768]{2,0,1:T(8,128)(2,1)}, bf16[4096,1,768]{2,0,1:T(8,128)(2,1)S(1)}, u32[]{:S(2)}, u32[]{:S(2)}) %collective-permute-start) | collective-permute-done | bytes 6291488 | tf_op jit(solution)/shard_map/ppermute | solution.py:12
  147.3 0.0 copy-start.2
  147.3 0.0 collective-permute-start.4
  147.3 0.0 slice-start
  147.3 0.0 slice-start.1
  147.3 3.8 collective-permute-start.3
  151.2 0.0 collective-permute-start.7
  151.2 8.6 %fusion.5 = f32[768,768]{1,0:T(8,128)} fusion(bf16[4096,1,768]{2,0,1:T(8,128)(2,1)S(1)} %collective-permute-done, bf16[4096,1,768]{2,0,1:T(8,128)(2,1)} %param.3), kind=kOutput, calls=%fused_computation.6 | convolution fusion | flops 4831838208 | bytes 14942208 | tf_op jit(solution)/shard_map/dot_general | solution.py:24
  159.8 0.0 copy-done.2
  159.8 0.0 copy-start.1
  159.8 127.8 %collective-permute-done.4 = bf16[4096,1,768]{2,0,1:T(8,128)(2,1)S(1)} collective-permute-done((bf16[4096,1,768]{2,0,1:T(8,128)(2,1)S(1)}, bf16[4096,1,768]{2,0,1:T(8,128)(2,1)S(1)}, u32[]{:S(2)}, u32[]{:S(2)}) %collective-permute-start.4) | collective-permute-done | bytes 6291488 | tf_op jit(solution)/shard_map/ppermute | solution.py:12
  287.5 0.0 copy-start
  287.5 2.7 copy-done
  290.2 0.0 slice-done
  290.2 0.0 slice-done.1
  290.2 6.6 fusion.1
  296.8 0.0 all-reduce.3.cloned.1.call-update
  296.8 266.7 %collective-permute-start.1 = (bf16[1]{0:T(256)(128)(2,1)}, bf16[1]{0:T(256)(128)(2,1)}, u32[]{:S(2)}, u32[]{:S(2)}) collective-permute-start(bf16[1]{0:T(256)(128)(2,1)} %param.4), channel_id=1, source_target_pairs={{12,0},{0,4},{4,8},{8,12},{13,1},{1,5},{5,9},{9,13},{14,2},{2,6},{... | collective-permute-start | bytes 14 | tf_op jit(solution)/shard_map/ppermute | solution.py:12
  564.3 0.7 collective-permute-done.1
  565.6 122.2 %collective-permute-start.5 = (bf16[1]{0:T(256)(128)(2,1)}, bf16[1]{0:T(256)(128)(2,1)}, u32[]{:S(2)}, u32[]{:S(2)}) collective-permute-start(bf16[1]{0:T(256)(128)(2,1)} %collective-permute-done.1), channel_id=1, source_target_pairs={{12,0},{0,4},{4,8},{8,12},{13,1},{1,5},{5,9},{9,13},{14,2},{2,6},{... | collective-permute-start | bytes 14 | tf_op jit(solution)/shard_map/ppermute | solution.py:12
  687.8 1.5 collective-permute-done.5
  689.9 0.0 copy-done.1
  689.9 0.0 all-reduce.3.cloned.1.call-done
  689.9 0.0 copy-start.3
  690.0 3.3 divide_convert_fusion.1
  693.3 3.8 collective-permute-start.2
  697.1 0.6 collective-permute-start.6
  697.8 0.0 copy-done.3
  697.8 7.9 fusion.3
  705.7 0.0 collective-permute-done.7
  705.7 65.2 %collective-permute-done.6 = bf16[768,768]{1,0:T(8,128)(2,1)S(1)} collective-permute-done((bf16[768,768]{1,0:T(8,128)(2,1)S(1)}, bf16[768,768]{1,0:T(8,128)(2,1)S(1)}, u32[]{:S(2)}, u32[]{:S(2)}) %collective-permute-start.6) | collective-permute-done | bytes 1179680 | tf_op jit(solution)/shard_map/ppermute | solution.py:12
  770.9 10.8 %fusion.13 = f32[768,4096]{1,0:T(8,128)} fusion(bf16[768,768]{1,0:T(8,128)(2,1)S(1)} %collective-permute-done.6, bf16[4096,768]{1,0:T(8,128)(2,1)} %collective-permute-done.7), kind=kOutput, calls=%fused_computation.17 | convolution fusion | flops 4831838208 | bytes 20054016 | tf_op jit(solution)/shard_map/dot_general | solution.py:56
  781.7 0.0 collective-permute-done.3
  781.7 0.0 collective-permute-done.2
  781.7 11.0 %fusion.12 = f32[768,4096]{1,0:T(8,128)} fusion(bf16[768,768]{1,0:T(8,128)(2,1)S(1)} %collective-permute-done.2, bf16[4096,768]{1,0:T(8,128)(2,1)} %collective-permute-done.3), kind=kOutput, calls=%fused_computation.16 | convolution fusion | flops 4831838208 | bytes 20054016 | tf_op jit(solution)/shard_map/dot_general | solution.py:48
  792.7 19.1 %fusion.7 = bf16[4096,1,768]{0,2,1:T(8,128)(2,1)} fusion(f32[768,4096]{1,0:T(8,128)} %fusion.13, bf16[768,768]{1,0:T(8,128)(2,1)S(1)} %get-tuple-element.8, bf16[4096,1,768]{2,0,1:T(8,128)(2,1)} %copy-done, f32[768,4096]{1,0:T(8,128)} %fusion.3, f32[768,4096]{1,0:T(8,128)} %fusion.12), kind=kOutput, calls=%fused_computation.8 | convolution fusion | flops 4844421120 | bytes 51511296 | tf_op jit(solution)/shard_map/dot_general | solution.py:52
  811.8 8.6 %copy.4 = bf16[4096,1,768]{2,0,1:T(8,128)(2,1)} copy(bf16[4096,1,768]{0,2,1:T(8,128)(2,1)} %fusion.7) | data formatting | bytes 12582912 | tf_op jit(solution)/shard_map/reshape | solution.py:57
  (2 shorter events, 0.0 us)
Async XLA Ops:
  6.5 683.4 %all-reduce.3.cloned.1.call-start = ((), (), s32[]{:S(2)}) async-start(), calls=%async_computation | async-start | bytes 9437184 | tf_op jit(solution)/shard_map/psum | solution.py:27
  6.5 140.8 %collective-permute-start = (bf16[4096,1,768]{2,0,1:T(8,128)(2,1)}, bf16[4096,1,768]{2,0,1:T(8,128)(2,1)S(1)}, u32[]{:S(2)}, u32[]{:S(2)}) collective-permute-start(bf16[4096,1,768]{2,0,1:T(8,128)(2,1)} %param.3), channel_id=1, source_target_pairs={{12,0},{0,4},{4,8},{8,12},{13,1},{1,5},{5,9},{9,13},{14,2},{2,6},{... | collective-permute-start | bytes 18874376 | tf_op jit(solution)/shard_map/ppermute | solution.py:12
  147.3 12.4 %copy-start.2 = (bf16[4096,1,768]{2,0,1:T(8,128)(2,1)}, bf16[4096,1,768]{2,0,1:T(8,128)(2,1)S(1)}, u32[]{:S(2)}) copy-start(bf16[4096,1,768]{2,0,1:T(8,128)(2,1)S(1)} %collective-permute-done) | copy-start | bytes 18874372
  147.3 140.2 %collective-permute-start.4 = (bf16[4096,1,768]{2,0,1:T(8,128)(2,1)S(1)}, bf16[4096,1,768]{2,0,1:T(8,128)(2,1)S(1)}, u32[]{:S(2)}, u32[]{:S(2)}) collective-permute-start(bf16[4096,1,768]{2,0,1:T(8,128)(2,1)S(1)} %collective-permute-done), channel_id=1, source_target_pairs={{12,0},{0,4},{4,8},{8,12},{13,1},{1,5},{5,9},{9,13},{14,2},{2,6},{... | collective-permute-start | bytes 18874376 | tf_op jit(solution)/shard_map/ppermute | solution.py:12
  147.3 142.9 %slice-start = ((s8[6291456]{0:T(1024)(128)(4,1)}), s8[4194304]{0:T(1024)(128)(4,1)S(1)}, s32[]{:S(2)}) async-start(s8[6291456]{0:T(1024)(128)(4,1)} %bitcast.36), calls=%async_computation.1 | async-start | bytes 8388608
  147.3 142.9 %slice-start.1 = ((s8[6291456]{0:T(1024)(128)(4,1)}), s8[2097152]{0:T(1024)(128)(4,1)S(1)}, s32[]{:S(2)}) async-start(s8[6291456]{0:T(1024)(128)(4,1)} %bitcast.36), calls=%async_computation.2 | async-start | bytes 4194304
  147.3 634.4 %collective-permute-start.3 = (bf16[4096,768]{1,0:T(8,128)(2,1)}, bf16[4096,768]{1,0:T(8,128)(2,1)}, u32[]{:S(2)}, u32[]{:S(2)}) collective-permute-start(bf16[4096,768]{1,0:T(8,128)(2,1)} %bitcast.34), channel_id=1, source_target_pairs={{4,0},{8,4},{12,8},{0,12},{5,1},{9,5},{13,9},{1,13},{6,2},{10,6},{... | collective-permute-start | bytes 18874376 | tf_op jit(solution)/shard_map/ppermute | solution.py:12
  151.2 554.5 %collective-permute-start.7 = (bf16[4096,768]{1,0:T(8,128)(2,1)}, bf16[4096,768]{1,0:T(8,128)(2,1)}, u32[]{:S(2)}, u32[]{:S(2)}) collective-permute-start(bf16[4096,768]{1,0:T(8,128)(2,1)} %bitcast.35), channel_id=1, source_target_pairs={{8,0},{12,4},{0,8},{4,12},{9,1},{13,5},{1,9},{5,13},{10,2},{14,6},... | collective-permute-start | bytes 18874376 | tf_op jit(solution)/shard_map/ppermute | solution.py:12
  159.8 530.1 %copy-start.1 = (f32[768]{0:T(1024)S(1)}, f32[768]{0:T(1024)}, u32[]{:S(2)}) copy-start(f32[768]{0:T(1024)} %param.5) | copy-start | bytes 9220
  287.5 2.7 copy-start
  296.8 268.1 %collective-permute-start.1 = (bf16[1]{0:T(256)(128)(2,1)}, bf16[1]{0:T(256)(128)(2,1)}, u32[]{:S(2)}, u32[]{:S(2)}) collective-permute-start(bf16[1]{0:T(256)(128)(2,1)} %param.4), channel_id=1, source_target_pairs={{12,0},{0,4},{4,8},{8,12},{13,1},{1,5},{5,9},{9,13},{14,2},{2,6},{... | collective-permute-start | bytes 14 | tf_op jit(solution)/shard_map/ppermute | solution.py:12
  565.6 123.7 %collective-permute-start.5 = (bf16[1]{0:T(256)(128)(2,1)}, bf16[1]{0:T(256)(128)(2,1)}, u32[]{:S(2)}, u32[]{:S(2)}) collective-permute-start(bf16[1]{0:T(256)(128)(2,1)} %collective-permute-done.1), channel_id=1, source_target_pairs={{12,0},{0,4},{4,8},{8,12},{13,1},{1,5},{5,9},{9,13},{14,2},{2,6},{... | collective-permute-start | bytes 14 | tf_op jit(solution)/shard_map/ppermute | solution.py:12
  689.9 7.8 copy-start.3
  693.3 88.4 %collective-permute-start.2 = (bf16[768,768]{1,0:T(8,128)(2,1)S(1)}, bf16[768,768]{1,0:T(8,128)(2,1)S(1)}, u32[]{:S(2)}, u32[]{:S(2)}) collective-permute-start(bf16[768,768]{1,0:T(8,128)(2,1)S(1)} %get-tuple-element.7), channel_id=1, source_target_pairs={{4,0},{8,4},{12,8},{0,12},{5,1},{9,5},{13,9},{1,13},{6,2},{10,6},{... | collective-permute-start | bytes 3538952 | tf_op jit(solution)/shard_map/ppermute | solution.py:12
  697.1 73.8 %collective-permute-start.6 = (bf16[768,768]{1,0:T(8,128)(2,1)S(1)}, bf16[768,768]{1,0:T(8,128)(2,1)S(1)}, u32[]{:S(2)}, u32[]{:S(2)}) collective-permute-start(bf16[768,768]{1,0:T(8,128)(2,1)S(1)} %get-tuple-element.8), channel_id=1, source_target_pairs={{8,0},{12,4},{0,8},{4,12},{9,1},{13,5},{1,9},{5,13},{10,2},{14,6},... | collective-permute-start | bytes 3538952 | tf_op jit(solution)/shard_map/ppermute | solution.py:12
Sparse Core Ops, SparseCore 0:
  297.0 360.2 all-reduce.2
where the time goes:
time: 828 us; the launch traced here: 827 us
  starting transfers between devices  400 us (48%)
  waiting for transfers between devices  333 us (40%)
  matrix products  64 us (8%)
  between operations  15.3 us (2%)
  local copies, waits for them, and re-layouts  11.3 us (1%)
    ppermute x8, starting transfers between devices, shifted(): return lax.ppermute(block, axis, route)  400 us
    ppermute x8, waiting for transfers between devices, shifted(): return lax.ppermute(block, axis, route)  333 us
    dot_general x1, matrix products, on_device(): lax.dot_general(second_block, second_amplitude, (((1,), (1,)), ((), ())),...  19.1 us
  transfers between devices with their start and end apart: 9, of which 5 were waited for; matrix products, arithmetic and copies ran while one was open for 5% of the time, Pallas kernels for 0%

commit v1 on v0

--- a/solution.py
+++ b/solution.py
@@ -1,9 +1,17 @@
+import functools
+
 import jax
 import jax.numpy as jnp
 from jax import lax
+from jax.experimental import pallas as pl
+from jax.experimental.pallas import tpu as pltpu
 from jax.sharding import PartitionSpec as P
 
 spin_scale = 1.2
+MESH = pl.DeviceIdType.MESH
+CHUNKS = 8
+WIDE = 256
+F32, BF16 = jnp.float32, jnp.bfloat16
 
 
 def shifted(block, axis, distance):
@@ -29,7 +37,7 @@
     return (spin_scale * pair_sums / denominator).astype(jnp.bfloat16)
 
 
-def on_device(three_index, occupied_energy, virtual_energy):
+def any_cycle(three_index, occupied_energy, virtual_energy):
     aux_rows, occ_rows, slab_size = three_index.shape
     own_block = three_index.reshape(aux_rows, occ_rows * slab_size)
     first_index, first_energy = shifted((three_index, occupied_energy), "occ", 1)
@@ -57,8 +65,259 @@
     return accumulated.astype(jnp.bfloat16).reshape(aux_rows, occ_rows, slab_size)
 
 
+OI, OJ, IJ, OK = range(4)
+
+
+def four_blocks(x, e_own, e_row, e_col, out, o_buf, j_buf, k_buf, stage_o, stage_i, g, t, t_ki,
+                z_out, z_in, c_out, c_in, x_out, x_in, e_buf,
+                o_s, o_r, j_s, j_r, k_s, k_r, res_s, res_r, e_s, e_r, z_s, z_r,
+                c_s, c_r, x_s, x_r, t_s, t_r, ki_s, ki_r, out_s):
+    rows, width = x.shape
+    size, half = rows // CHUNKS, width // 2
+    v, z, a = lax.axis_index("virt"), lax.axis_index("occ"), lax.axis_index("aux")
+    core = lax.rem(a, 2)
+    inner = jnp.logical_or(z == 1, z == 2)
+    outer = jnp.logical_or(z == 0, z == 3)
+    mate_z = z + 1 - 2 * lax.rem(z, 2)
+    mate, mirror = (v, mate_z, a), (v, 3 - z, a)
+    core_mate, x_mate = (v, z, a + 1 - 2 * core), (v, z, lax.rem(a + 2, 4))
+    around = [(v, lax.rem(z + d, 4), a) for d in (1, 2, 3)]
+
+    barrier = pltpu.get_barrier_semaphore()
+    for peer in around + [core_mate, x_mate]:
+        pl.semaphore_signal(barrier, inc=1, device_id=peer, device_id_type=MESH)
+    pl.semaphore_wait(barrier, 5)
+
+    def remote(src, dst, send, recv, peer):
+        return pltpu.make_async_remote_copy(
+            src_ref=src, dst_ref=dst, send_sem=send, recv_sem=recv, device_id=peer,
+            device_id_type=MESH)
+
+    def part(c):
+        return pl.ds(pl.multiple_of(c * size, size), size)
+
+    energies = [remote(e_own, e_buf.at[d], e_s.at[d], e_r.at[d], around[d]) for d in range(3)]
+    for copy in energies:
+        copy.start()
+
+    def o_copy(c):
+        return remote(x.at[part(c)], o_buf.at[part(c)], o_s.at[c], o_r.at[c], mate)
+
+    def j_copy(c):
+        return remote(x.at[part(c)], j_buf.at[part(c)], j_s.at[c], j_r.at[c], mirror)
+
+    def k_copy(c):
+        return remote(o_buf.at[part(c)], k_buf.at[part(c)], k_s.at[c], k_r.at[c], mirror)
+
+    def res_copy(c):
+        return remote(stage_o.at[lax.rem(c, 2)], o_buf.at[part(c)], res_s.at[c], res_r.at[c], mate)
+
+    def out_copy(c):
+        return pltpu.make_async_copy(stage_i.at[lax.rem(c, 2)], out.at[part(c)],
+                                     out_s.at[lax.rem(c, 2)])
+
+    def gram(pair, left, right, c):
+        @pl.loop(0, width // WIDE)
+        def _(n):
+            cols = pl.ds(pl.multiple_of(n * WIDE, WIDE), WIDE)
+            g[pair, :, cols] += lax.dot_general(
+                left[part(c), :], right[part(c), cols], (((0,), (0,)), ((), ())),
+                preferred_element_type=F32)
+
+    for copy in energies:
+        copy.wait()
+
+    @pl.when(outer)
+    def _():
+        @pl.loop(0, CHUNKS)
+        def _(c):
+            o_copy(c).start()
+
+        @pl.loop(0, CHUNKS)
+        def _(c):
+            res_copy(c).wait_recv()
+            pltpu.make_async_copy(o_buf.at[part(c)], out.at[part(c)], out_s.at[0]).start()
+            pltpu.make_async_copy(o_buf.at[part(c)], out.at[part(c)], out_s.at[0]).wait()
+
+        @pl.loop(0, CHUNKS)
+        def _(c):
+            o_copy(c).wait_send()
+
+    @pl.when(inner)
+    def _():
+        @pl.loop(0, CHUNKS)
+        def _(c):
+            j_copy(c).start()
+
+        g[...] = jnp.zeros_like(g)
+
+        @pl.loop(0, CHUNKS)
+        def _(c):
+            o_copy(c).wait_recv()
+            j_copy(c).wait_recv()
+            gram(OI, o_buf, x, c)
+            gram(OJ, o_buf, j_buf, c)
+            gram(IJ, x, j_buf, c)
+
+        first = jnp.where(z == 1, CHUNKS // 2, 0)
+
+        @pl.loop(0, CHUNKS)
+        def _(c):
+            j_copy(c).wait_send()
+            k_copy(lax.rem(c + first, CHUNKS)).start()
+
+        mine = pl.ds(pl.multiple_of(core * half, half), half)
+        other = pl.ds(pl.multiple_of(half - core * half, half), half)
+        e_i = e_own[0:1, 0:1]
+
+        def occupied(block):
+            slot = lax.rem(z - block + 3, 4)
+            return e_buf[slot][0:1, 0:1]
+
+        e_o, e_j, e_k = occupied(mate_z), occupied(3 - z), occupied(3 - mate_z)
+
+        def core_copy(p):
+            return remote(c_out.at[p], c_in.at[p], c_s.at[p], c_r.at[p], core_mate)
+
+        def x_copy(p):
+            return remote(x_out.at[p], x_in.at[p], x_s.at[p], x_r.at[p], x_mate)
+
+        def t_copy(p):
+            return remote(t.at[p, mine], t.at[p, mine], t_s.at[p], t_r.at[p], core_mate)
+
+        def reduce(pairs):
+            for p, _, _, _ in pairs:
+                c_out[p] = g[p, other, :].astype(BF16)
+                core_copy(p).start()
+            for p, _, _, _ in pairs:
+                core_copy(p).wait()
+                x_out[p] = (g[p, mine, :] + c_in[p].astype(F32)).astype(BF16)
+                x_copy(p).start()
+            for p, left, right, weight in pairs:
+                x_copy(p).wait()
+                sums = x_out[p].astype(F32) + x_in[p].astype(F32)
+                levels = (e_col[mine, :] - left) + (e_row[...] - right)
+                t[p, mine, :] = ((spin_scale * sums / levels).astype(BF16).astype(F32)
+                                 * weight).astype(BF16)
+                t_copy(p).start()
+            for p, _, _, _ in pairs:
+                t_copy(p).wait()
+
+        reduce([(OJ, e_o, e_j, 2.0), (OI, e_o, e_i, 1.0), (IJ, e_i, e_j, 1.0)])
+        ki_copy = remote(t.at[OJ], t_ki, ki_s, ki_r, mirror)
+        ki_copy.start()
+
+        @pl.loop(0, CHUNKS // 2)
+        def _(c):
+            at = jnp.where(z == 1, c, c + CHUNKS // 2)
+            k_copy(at).wait_recv()
+            gram(OK, o_buf, k_buf, at)
+
+        z_out[...] = g[OK].astype(BF16)
+        z_copy = remote(z_out, z_in, z_s, z_r, mirror)
+        z_copy.start()
+        z_copy.wait()
+        g[OK] += z_in[...].T.astype(F32)
+        reduce([(OK, e_o, e_k, 1.0)])
+        ki_copy.wait()
+
+        nt = (((1,), (1,)), ((), ()))
+        nn = (((1,), (0,)), ((), ()))
+
+        def product(left, right, dims):
+            return lax.dot_general(left, right, dims, preferred_element_type=F32)
+
+        @pl.loop(0, CHUNKS)
+        def _(c):
+            at = jnp.where(z == 1, c, lax.rem(c + CHUNKS // 2, CHUNKS))
+            before = jnp.where(z == 1, c - 2, lax.rem(c + CHUNKS // 2 - 2, CHUNKS))
+            slot = lax.rem(c, 2)
+
+            @pl.when(c >= CHUNKS // 2)
+            def _():
+                k_copy(at).wait_recv()
+
+            @pl.when(c >= 2)
+            def _():
+                res_copy(before).wait_send()
+                out_copy(before).wait()
+
+            @pl.loop(0, width // WIDE)
+            def _(n):
+                cols = pl.ds(pl.multiple_of(n * WIDE, WIDE), WIDE)
+                stage_o[slot, :, cols] = (
+                    product(x[part(at), :], t[OI, cols, :], nt)
+                    + product(j_buf[part(at), :], t[OJ, cols, :], nt)
+                    + product(k_buf[part(at), :], t[OK, cols, :], nt)).astype(BF16)
+
+            res_copy(at).start()
+
+            @pl.loop(0, width // WIDE)
+            def _(n):
+                cols = pl.ds(pl.multiple_of(n * WIDE, WIDE), WIDE)
+                stage_i[slot, :, cols] = (
+                    product(o_buf[part(at), :], t[OI, :, cols], nn)
+                    + product(j_buf[part(at), :], t[IJ, cols, :], nt)
+                    + product(k_buf[part(at), :], t_ki[:, cols], nn)).astype(BF16)
+
+            out_copy(at).start()
+
+        @pl.loop(CHUNKS - 2, CHUNKS)
+        def _(c):
+            at = jnp.where(z == 1, c, lax.rem(c + CHUNKS // 2, CHUNKS))
+            res_copy(at).wait_send()
+            out_copy(at).wait()
+
+        @pl.loop(0, CHUNKS)
+        def _(c):
+            k_copy(c).wait_send()
+
+
+def cycle_of_four(three_index, occupied_energy, virtual_energy):
+    rows, _, width = three_index.shape
+    half = width // 2
+    pair = lambda n: pltpu.SemaphoreType.DMA((n,))
+    one = pltpu.SemaphoreType.DMA
+    scratch = [
+        pltpu.VMEM((rows, width), BF16), pltpu.VMEM((rows, width), BF16),
+        pltpu.VMEM((rows, width), BF16),
+        pltpu.VMEM((2, rows // CHUNKS, width), BF16), pltpu.VMEM((2, rows // CHUNKS, width), BF16),
+        pltpu.VMEM((4, width, width), F32), pltpu.VMEM((4, width, width), BF16),
+        pltpu.VMEM((width, width), BF16), pltpu.VMEM((width, width), BF16),
+        pltpu.VMEM((width, width), BF16),
+        pltpu.VMEM((4, half, width), BF16), pltpu.VMEM((4, half, width), BF16),
+        pltpu.VMEM((4, half, width), BF16), pltpu.VMEM((4, half, width), BF16),
+        pltpu.VMEM((3, 8, 128), F32),
+        pair(CHUNKS), pair(CHUNKS), pair(CHUNKS), pair(CHUNKS), pair(CHUNKS), pair(CHUNKS),
+        pair(CHUNKS), pair(CHUNKS), pair(3), pair(3), one, one,
+        pair(4), pair(4), pair(4), pair(4), pair(4), pair(4), one, one, pair(2),
+    ]
+    vmem = pl.BlockSpec(memory_space=pltpu.VMEM)
+    density = pl.pallas_call(
+        four_blocks,
+        out_shape=jax.ShapeDtypeStruct((rows, width), BF16),
+        in_specs=[vmem] * 4,
+        out_specs=pl.BlockSpec(memory_space=pl.ANY),
+        scratch_shapes=scratch,
+        compiler_params=pltpu.CompilerParams(
+            collective_id=0, has_side_effects=True, vmem_limit_bytes=67_000_000),
+    )(
+        three_index.reshape(rows, width),
+        jnp.broadcast_to(occupied_energy.astype(F32)[:, None], (8, 128)),
+        virtual_energy[None, :],
+        virtual_energy[:, None],
+    )
+    return density.reshape(rows, 1, width)
+
+
 def solution(mesh):
     placed = (P("aux", "occ", "virt"), P("occ"), P("virt"))
+
+    def on_device(three_index, occupied_energy, virtual_energy):
+        paired = mesh.shape["occ"] == 4 and mesh.shape["aux"] == 4 and three_index.shape[1] == 1
+        body = cycle_of_four if paired else any_cycle
+        return body(three_index, occupied_energy, virtual_energy)
+
     return jax.shard_map(
         on_device, mesh=mesh, in_specs=placed, out_specs=P("aux", "occ", "virt"), check_vma=False
     )

time: 828 us -> 507 us (0.61)
  Pallas kernels: 0 us -> 497 us
  starting transfers between devices: 400 us -> 0 us
  waiting for transfers between devices: 333 us -> 0 us
  matrix products: 64 us -> 0 us
  between operations: 15.3 us -> 0.67 us
    pallas_call x0 -> x1, Pallas kernels: none -> 497 us  [cycle_of_four(): pl.pallas_call(four_blocks, out_shape=jax.ShapeDtypeStruct((rows, width),...]
    ppermute x8 -> x0, starting transfers between devices: 400 us -> none  [shifted(): return lax.ppermute(block, axis, route)]
    ppermute x8 -> x0, waiting for transfers between devices: 333 us -> none  [shifted(): return lax.ppermute(block, axis, route)]
    dot_general x6 -> x0, matrix products: 64 us -> none  [the longest x1 19.1 us: on_device(): lax.dot_general(second_block, second_amplitude, (((1,), (1,)), ((), ())),...]
    reshape x1 -> x0, local copies, waits for them, and re-layouts: 8.61 us -> none  [on_device(): accumulated.astype(jnp.bfloat16).reshape(aux_rows, occ_rows, slab_size)]
  transfers between devices with their start and end apart: 9 -> 0, of which waited for: 5 -> 0; matrix products, arithmetic and copies ran while one was open for 5% -> 0% of each run, Pallas kernels for 0% -> 0%
where the time goes in v1:
time: 507 us
  Pallas kernels  497 us (98%)
  local copies, waits for them, and re-layouts  9.36 us (2%)
    pallas_call x1, Pallas kernels, cycle_of_four(): pl.pallas_call(four_blocks, out_shape=jax.ShapeDtypeStruct((rows, width),...  497 us

profile of v1, /device:TPU:0, one launch (start us, length us, event | category | flops | bytes accessed | tf_op | source)
XLA Modules:
  0.0 506.9 jit_solution(12138510595683562094)
XLA Ops:
  0.7 1.3 broadcast_in_dim.20.e_row
  1.9 0.6 broadcast_in_dim.19.e_own
  2.5 1.6 broadcast_in_dim.23.e_col
  4.1 496.9 %shard_map.37 = bf16[4096,768]{1,0:T(8,128)(2,1)} custom-call(bf16[4096,768]{1,0:T(8,128)(2,1)} %bitcast.6, f32[8,128]{1,0:T(8,128)} %broadcast_in_dim.19.e_own, f32[1,768]{1,0:T(1,128)} %broadcast_in_dim.20.e_row, f32[768,1]{1,0:T(8,128)} %broadcast_in_dim.23.e_col), custom_call_target="tpu_custom_call" | custom-call | tf_op jit(solution)/shard_map/pallas_call | solution.py:296
  501.0 5.9 %copy.7 = bf16[4096,1,768]{2,0,1:T(8,128)(2,1)} copy(bf16[4096,1,768]{2,0,1:T(8,128)(2,1)} %bitcast.5) | data formatting | bytes 12582912

commit v2 on v0

--- a/solution.py
+++ b/solution.py
@@ -1,9 +1,17 @@
+import functools
+
 import jax
 import jax.numpy as jnp
 from jax import lax
+from jax.experimental import pallas as pl
+from jax.experimental.pallas import tpu as pltpu
 from jax.sharding import PartitionSpec as P
 
 spin_scale = 1.2
+MESH = pl.DeviceIdType.MESH
+CHUNKS = 8
+WIDE = 256
+F32, BF16 = jnp.float32, jnp.bfloat16
 
 
 def shifted(block, axis, distance):
@@ -29,7 +37,7 @@
     return (spin_scale * pair_sums / denominator).astype(jnp.bfloat16)
 
 
-def on_device(three_index, occupied_energy, virtual_energy):
+def any_cycle(three_index, occupied_energy, virtual_energy):
     aux_rows, occ_rows, slab_size = three_index.shape
     own_block = three_index.reshape(aux_rows, occ_rows * slab_size)
     first_index, first_energy = shifted((three_index, occupied_energy), "occ", 1)
@@ -57,8 +65,359 @@
     return accumulated.astype(jnp.bfloat16).reshape(aux_rows, occ_rows, slab_size)
 
 
+OI, OJ, IJ, OK, KI = range(5)
+
+
+def four_blocks(x, e_own, e_row, e_col, out, o_buf, j_buf, k_buf, stage_o, stage_i, g, t,
+                z_out, z_in, c_in, x_out, x_in, e_buf,
+                o_s, o_r, j_s, j_r, k_s, k_r, res_s, res_r, raw_s, raw_r, e_s, e_r, z_s, z_r,
+                c_s, c_r, x_s, x_r, t_s, t_r, go_s, go_r, ki_s, ki_r, out_s):
+    rows, width = x.shape
+    size, half, early = rows // CHUNKS, width // 2, CHUNKS // 2
+    v, z, a = lax.axis_index("virt"), lax.axis_index("occ"), lax.axis_index("aux")
+    core = lax.rem(a, 2)
+    inner = jnp.logical_or(z == 1, z == 2)
+    outer = jnp.logical_or(z == 0, z == 3)
+    mate_z = z + 1 - 2 * lax.rem(z, 2)
+    mate, mirror = (v, mate_z, a), (v, 3 - z, a)
+    core_mate, x_mate = (v, z, a + 1 - 2 * core), (v, z, lax.rem(a + 2, 4))
+    around = [(v, lax.rem(z + d, 4), a) for d in (1, 2, 3)]
+    base = early * (z // 2)
+
+    barrier = pltpu.get_barrier_semaphore()
+    for peer in around + [core_mate, x_mate]:
+        pl.semaphore_signal(barrier, inc=1, device_id=peer, device_id_type=MESH)
+    pl.semaphore_wait(barrier, 5)
+
+    def remote(src, dst, send, recv, peer):
+        return pltpu.make_async_remote_copy(
+            src_ref=src, dst_ref=dst, send_sem=send, recv_sem=recv, device_id=peer,
+            device_id_type=MESH)
+
+    def turn(c):
+        return lax.rem(c + base, CHUNKS)
+
+    def part(at):
+        return pl.ds(pl.multiple_of(at * size, size), size)
+
+    def o_copy(at):
+        return remote(x.at[part(at)], o_buf.at[part(at)], o_s.at[at], o_r.at[at], mate)
+
+    def j_copy(at):
+        return remote(x.at[part(at)], j_buf.at[part(at)], j_s.at[at], j_r.at[at], mirror)
+
+    def k_copy(at):
+        return remote(o_buf.at[part(at)], k_buf.at[part(at)], k_s.at[at], k_r.at[at], mirror)
+
+    def raw_copy(kind, at):
+        src, dst = ((x, o_buf), (j_buf, j_buf), (k_buf, k_buf))[kind]
+        return remote(src.at[part(at)], dst.at[part(at)], raw_s.at[kind, at], raw_r.at[kind, at],
+                      mate)
+
+    def res_copy(at):
+        return remote(stage_o.at[lax.rem(at, 2)], o_buf.at[part(at)], res_s.at[at], res_r.at[at],
+                      mate)
+
+    def out_copy(at):
+        return pltpu.make_async_copy(stage_i.at[lax.rem(at, 2)], out.at[part(at)],
+                                     out_s.at[lax.rem(at, 2)])
+
+    def direct_copy(at):
+        return pltpu.make_async_copy(o_buf.at[part(at)], out.at[part(at)], out_s.at[2])
+
+    mine = pl.ds(pl.multiple_of(core * half, half), half)
+    other = pl.ds(pl.multiple_of(half - core * half, half), half)
+
+    def t_copy(p):
+        return remote(t.at[p, mine], t.at[p, mine], t_s.at[p], t_r.at[p], core_mate)
+
+    def go_copy(p):
+        return remote(t.at[p, mine], t.at[p, mine], go_s.at[p], go_r.at[p], mate)
+
+    nt = (((1,), (1,)), ((), ()))
+    nn = (((1,), (0,)), ((), ()))
+    tn = (((0,), (0,)), ((), ()))
+
+    def product(left, right, dims):
+        return lax.dot_general(left, right, dims, preferred_element_type=F32)
+
+    def wide_loop(body):
+        @pl.loop(0, width // WIDE)
+        def _(n):
+            body(pl.ds(pl.multiple_of(n * WIDE, WIDE), WIDE))
+
+    def outer_result(stage, slot, i_block, at):
+        def body(cols):
+            stage[slot, :, cols] = (
+                product(i_block[part(at), :], t[OI, cols, :], nt)
+                + product(j_buf[part(at), :], t[OJ, cols, :], nt)
+                + product(k_buf[part(at), :], t[OK, cols, :], nt)).astype(BF16)
+
+        wide_loop(body)
+
+    def gram(pair, left, right, at):
+        def body(cols):
+            g[pair, :, cols] += product(left[part(at), :], right[part(at), cols], tn)
+
+        wide_loop(body)
+
+    def turn_over():
+        @pl.when(z >= 2)
+        def _():
+            t[OK] = t[OK].T
+
+    energies = [remote(e_own, e_buf.at[d], e_s.at[d], e_r.at[d], around[d]) for d in range(3)]
+    for copy in energies:
+        copy.start()
+
+    @pl.when(outer)
+    def _():
+        @pl.loop(0, CHUNKS)
+        def _(c):
+            o_copy(turn(c)).start()
+
+        for p in (OJ, OI, OK):
+            go_copy(p).wait_recv()
+            t_copy(p).start()
+            t_copy(p).wait()
+        turn_over()
+
+        @pl.loop(0, early)
+        def _(c):
+            at = turn(c)
+            for kind in range(3):
+                raw_copy(kind, at).wait_recv()
+
+            @pl.when(c >= 2)
+            def _():
+                out_copy(turn(c - 2)).wait()
+
+            outer_result(stage_i, lax.rem(at, 2), o_buf, at)
+            out_copy(at).start()
+
+        @pl.loop(early, CHUNKS)
+        def _(c):
+            res_copy(turn(c)).wait_recv()
+            direct_copy(turn(c)).start()
+            direct_copy(turn(c)).wait()
+
+        @pl.loop(early - 2, early)
+        def _(c):
+            out_copy(turn(c)).wait()
+
+        @pl.loop(0, CHUNKS)
+        def _(c):
+            o_copy(c).wait_send()
+
+        for copy in energies:
+            copy.wait()
+
+    @pl.when(inner)
+    def _():
+        @pl.loop(0, CHUNKS)
+        def _(c):
+            j_copy(lax.rem(turn(c) + early, CHUNKS)).start()
+
+        @pl.loop(0, early)
+        def _(c):
+            raw_copy(0, turn(c)).start()
+
+        g[...] = jnp.zeros_like(g)
+
+        @pl.loop(0, CHUNKS)
+        def _(c):
+            at = turn(c)
+            j_copy(at).wait_recv()
+
+            @pl.when(c < early)
+            def _():
+                raw_copy(1, at).start()
+
+            o_copy(at).wait_recv()
+
+            @pl.when(c >= early)
+            def _():
+                k_copy(at).start()
+
+            gram(OI, o_buf, x, at)
+            gram(OJ, o_buf, j_buf, at)
+            gram(IJ, x, j_buf, at)
+
+        for copy in energies:
+            copy.wait()
+
+        def occupied(block):
+            return e_buf[lax.rem(z - block + 3, 4)][0:1, 0:1]
+
+        e_i = e_own[0:1, 0:1]
+        e_o, e_j, e_k = occupied(mate_z), occupied(3 - z), occupied(3 - mate_z)
+
+        def core_copy(p):
+            return remote(g.at[p, other], c_in.at[p], c_s.at[p], c_r.at[p], core_mate)
+
+        def x_copy(p):
+            return remote(x_out.at[p], x_in.at[p], x_s.at[p], x_r.at[p], x_mate)
+
+        def finish(p, left, right, weight):
+            x_copy(p).wait()
+            sums = g[p, mine, :] + x_in[p].astype(F32)
+            levels = (e_col[mine, :] - left) + (e_row[...] - right)
+            t[p, mine, :] = ((spin_scale * sums / levels).astype(BF16).astype(F32)
+                             * weight).astype(BF16)
+            t_copy(p).start()
+
+        for p in (OJ, OI, IJ):
+            core_copy(p).start()
+        for p in (OJ, OI, IJ):
+            core_copy(p).wait()
+            g[p, mine, :] += c_in[p]
+            x_out[p] = g[p, mine, :].astype(BF16)
+            x_copy(p).start()
+
+        def far_pair(c):
+            at = turn(c)
+            k_copy(at).wait_recv()
+            raw_copy(2, at).start()
+
+            @pl.when(z == 1)
+            def _():
+                gram(OK, o_buf, k_buf, at)
+
+            @pl.when(z == 2)
+            def _():
+                gram(OK, k_buf, o_buf, at)
+
+        @pl.loop(0, early - 2)
+        def _(c):
+            far_pair(c)
+
+        ki_copy = remote(t.at[OJ, mine], t.at[KI, mine], ki_s, ki_r, mirror)
+        finish(OJ, e_o, e_j, 2.0)
+        go_copy(OJ).start()
+        ki_copy.start()
+        finish(OI, e_o, e_i, 1.0)
+        go_copy(OI).start()
+        far_pair(early - 2)
+        finish(IJ, e_i, e_j, 1.0)
+        far_pair(early - 1)
+
+        core_copy(OK).start()
+        core_copy(OK).wait()
+        g[OK, mine, :] += c_in[OK]
+        z_out[...] = g[OK, mine, :].astype(BF16)
+        z_copy = remote(z_out, z_in, z_s, z_r, mirror)
+        z_copy.start()
+
+        @pl.loop(0, early)
+        def _(c):
+            k_copy(turn(c)).start()
+
+        z_copy.wait()
+        g[OK, mine, :] += z_in[...].astype(F32)
+        x_out[OK] = g[OK, mine, :].astype(BF16)
+        x_copy(OK).start()
+        ki_copy.wait()
+        t_copy(KI).start()
+        finish(OK, jnp.where(z == 1, e_o, e_k), jnp.where(z == 1, e_k, e_o), 1.0)
+        go_copy(OK).start()
+        for p in (OJ, OI, IJ, KI, OK):
+            t_copy(p).wait()
+        for p in (OJ, OI, OK):
+            go_copy(p).wait_send()
+        turn_over()
+
+        def inner_result(at):
+            slot = lax.rem(at, 2)
+
+            def body(cols):
+                stage_i[slot, :, cols] = (
+                    product(o_buf[part(at), :], t[OI, :, cols], nn)
+                    + product(j_buf[part(at), :], t[IJ, cols, :], nt)
+                    + product(k_buf[part(at), :], t[KI, :, cols], nn)).astype(BF16)
+
+            wide_loop(body)
+
+        @pl.loop(0, CHUNKS)
+        def _(c):
+            at = turn(lax.rem(c + early, CHUNKS))
+
+            @pl.when(c < early)
+            def _():
+                k_copy(at).wait_recv()
+
+                @pl.when(c >= 2)
+                def _():
+                    res_copy(turn(c + early - 2)).wait_send()
+
+                outer_result(stage_o, lax.rem(at, 2), x, at)
+                res_copy(at).start()
+
+            @pl.when(c >= 2)
+            def _():
+                out_copy(turn(lax.rem(c + early - 2, CHUNKS))).wait()
+
+            inner_result(at)
+            out_copy(at).start()
+
+        @pl.loop(CHUNKS - 2, CHUNKS)
+        def _(c):
+            out_copy(turn(c - early)).wait()
+            res_copy(turn(c)).wait_send()
+
+        @pl.loop(0, CHUNKS)
+        def _(c):
+            j_copy(c).wait_send()
+            k_copy(c).wait_send()
+
+        @pl.loop(0, early)
+        def _(c):
+            for kind in range(3):
+                raw_copy(kind, turn(c)).wait_send()
+
+
+def cycle_of_four(three_index, occupied_energy, virtual_energy):
+    rows, _, width = three_index.shape
+    half = width // 2
+    size = rows // CHUNKS
+    flags = pltpu.SemaphoreType.DMA
+    scratch = [
+        pltpu.VMEM((rows, width), BF16), pltpu.VMEM((rows, width), BF16),
+        pltpu.VMEM((rows, width), BF16),
+        pltpu.VMEM((2, size, width), BF16), pltpu.VMEM((2, size, width), BF16),
+        pltpu.VMEM((4, width, width), F32), pltpu.VMEM((5, width, width), BF16),
+        pltpu.VMEM((half, width), BF16), pltpu.VMEM((half, width), BF16),
+        pltpu.VMEM((4, half, width), F32),
+        pltpu.VMEM((4, half, width), BF16), pltpu.VMEM((4, half, width), BF16),
+        pltpu.VMEM((3, 8, 128), F32),
+    ]
+    scratch += [flags((CHUNKS,))] * 8 + [flags((3, CHUNKS))] * 2 + [flags((3,))] * 2 + [flags] * 2
+    scratch += [flags((4,))] * 4 + [flags((5,))] * 4 + [flags] * 2 + [flags((3,))]
+    vmem = pl.BlockSpec(memory_space=pltpu.VMEM)
+    density = pl.pallas_call(
+        four_blocks,
+        out_shape=jax.ShapeDtypeStruct((rows, width), BF16),
+        in_specs=[vmem] * 4,
+        out_specs=pl.BlockSpec(memory_space=pl.ANY),
+        scratch_shapes=scratch,
+        compiler_params=pltpu.CompilerParams(
+            collective_id=0, has_side_effects=True, vmem_limit_bytes=67_000_000),
+    )(
+        three_index.reshape(rows, width),
+        jnp.broadcast_to(occupied_energy.astype(F32)[:, None], (8, 128)),
+        virtual_energy[None, :],
+        virtual_energy[:, None],
+    )
+    return density.reshape(rows, 1, width)
+
+
 def solution(mesh):
     placed = (P("aux", "occ", "virt"), P("occ"), P("virt"))
+
+    def on_device(three_index, occupied_energy, virtual_energy):
+        paired = mesh.shape["occ"] == 4 and mesh.shape["aux"] == 4 and three_index.shape[1] == 1
+        body = cycle_of_four if paired else any_cycle
+        return body(three_index, occupied_energy, virtual_energy)
+
     return jax.shard_map(
         on_device, mesh=mesh, in_specs=placed, out_specs=P("aux", "occ", "virt"), check_vma=False
     )

time: 828 us -> 347 us (0.42)
  starting transfers between devices: 400 us -> 0 us
  Pallas kernels: 0 us -> 337 us
  waiting for transfers between devices: 333 us -> 0 us
  matrix products: 64 us -> 0 us
  between operations: 15.3 us -> 0.67 us
    ppermute x8 -> x0, starting transfers between devices: 400 us -> none  [shifted(): return lax.ppermute(block, axis, route)]
    pallas_call x0 -> x1, Pallas kernels: none -> 337 us  [cycle_of_four(): pl.pallas_call(four_blocks, out_shape=jax.ShapeDtypeStruct((rows, width),...]
    ppermute x8 -> x0, waiting for transfers between devices: 333 us -> none  [shifted(): return lax.ppermute(block, axis, route)]
    dot_general x6 -> x0, matrix products: 64 us -> none  [the longest x1 19.1 us: on_device(): lax.dot_general(second_block, second_amplitude, (((1,), (1,)), ((), ())),...]
    reshape x1 -> x0, local copies, waits for them, and re-layouts: 8.61 us -> none  [on_device(): accumulated.astype(jnp.bfloat16).reshape(aux_rows, occ_rows, slab_size)]
  transfers between devices with their start and end apart: 9 -> 0, of which waited for: 5 -> 0; matrix products, arithmetic and copies ran while one was open for 5% -> 0% of each run, Pallas kernels for 0% -> 0%
where the time goes in v2:
time: 347 us
  Pallas kernels  337 us (97%)
  local copies, waits for them, and re-layouts  9.36 us (3%)
    pallas_call x1, Pallas kernels, cycle_of_four(): pl.pallas_call(four_blocks, out_shape=jax.ShapeDtypeStruct((rows, width),...  337 us

profile of v2, /device:TPU:0, one launch (start us, length us, event | category | flops | bytes accessed | tf_op | source)
XLA Modules:
  0.0 346.8 jit_solution(5165646129676740821)
XLA Ops:
  0.7 1.3 broadcast_in_dim.20.e_row
  1.9 0.6 broadcast_in_dim.19.e_own
  2.5 1.6 broadcast_in_dim.23.e_col
  4.1 336.8 %shard_map.37 = bf16[4096,768]{1,0:T(8,128)(2,1)} custom-call(bf16[4096,768]{1,0:T(8,128)(2,1)} %bitcast.6, f32[8,128]{1,0:T(8,128)} %broadcast_in_dim.19.e_own, f32[1,768]{1,0:T(1,128)} %broadcast_in_dim.20.e_row, f32[768,1]{1,0:T(8,128)} %broadcast_in_dim.23.e_col), custom_call_target="tpu_custom_call" | custom-call | tf_op jit(solution)/shard_map/pallas_call | solution.py:396
  340.9 5.9 %copy.7 = bf16[4096,1,768]{2,0,1:T(8,128)(2,1)} copy(bf16[4096,1,768]{2,0,1:T(8,128)(2,1)} %bitcast.5) | data formatting | bytes 12582912

commit v3 on v2

--- a/solution.py
+++ b/solution.py
@@ -9,7 +9,7 @@
 
 spin_scale = 1.2
 MESH = pl.DeviceIdType.MESH
-CHUNKS = 8
+CHUNKS = 16
 WIDE = 256
 F32, BF16 = jnp.float32, jnp.bfloat16
 
@@ -68,8 +68,8 @@
 OI, OJ, IJ, OK, KI = range(5)
 
 
-def four_blocks(x, e_own, e_row, e_col, out, o_buf, j_buf, k_buf, stage_o, stage_i, g, t,
-                z_out, z_in, c_in, x_out, x_in, e_buf,
+def four_blocks(x, e_own, e_row, out, o_buf, j_buf, k_buf, stage_o, stage_i, g, t,
+                z_out, z_in, c_in, x_out, x_in, e_col, e_buf,
                 o_s, o_r, j_s, j_r, k_s, k_r, res_s, res_r, raw_s, raw_r, e_s, e_r, z_s, z_r,
                 c_s, c_r, x_s, x_r, t_s, t_r, go_s, go_r, ki_s, ki_r, out_s):
     rows, width = x.shape
@@ -118,9 +118,8 @@
         return remote(stage_o.at[lax.rem(at, 2)], o_buf.at[part(at)], res_s.at[at], res_r.at[at],
                       mate)
 
-    def out_copy(at):
-        return pltpu.make_async_copy(stage_i.at[lax.rem(at, 2)], out.at[part(at)],
-                                     out_s.at[lax.rem(at, 2)])
+    def out_copy(at, slot):
+        return pltpu.make_async_copy(stage_i.at[slot], out.at[part(at)], out_s.at[slot])
 
     def direct_copy(at):
         return pltpu.make_async_copy(o_buf.at[part(at)], out.at[part(at)], out_s.at[2])
@@ -190,10 +189,10 @@
 
             @pl.when(c >= 2)
             def _():
-                out_copy(turn(c - 2)).wait()
+                out_copy(turn(c - 2), lax.rem(at, 2)).wait()
 
             outer_result(stage_i, lax.rem(at, 2), o_buf, at)
-            out_copy(at).start()
+            out_copy(at, lax.rem(at, 2)).start()
 
         @pl.loop(early, CHUNKS)
         def _(c):
@@ -203,7 +202,7 @@
 
         @pl.loop(early - 2, early)
         def _(c):
-            out_copy(turn(c)).wait()
+            out_copy(turn(c), lax.rem(c, 2)).wait()
 
         @pl.loop(0, CHUNKS)
         def _(c):
@@ -223,6 +222,7 @@
             raw_copy(0, turn(c)).start()
 
         g[...] = jnp.zeros_like(g)
+        e_col[...] = jnp.broadcast_to(e_row[...], (8, width)).T
 
         @pl.loop(0, CHUNKS)
         def _(c):
@@ -261,7 +261,7 @@
         def finish(p, left, right, weight):
             x_copy(p).wait()
             sums = g[p, mine, :] + x_in[p].astype(F32)
-            levels = (e_col[mine, :] - left) + (e_row[...] - right)
+            levels = (e_col[mine, 0:1] - left) + (e_row[...] - right)
             t[p, mine, :] = ((spin_scale * sums / levels).astype(BF16).astype(F32)
                              * weight).astype(BF16)
             t_copy(p).start()
@@ -299,6 +299,7 @@
         go_copy(OI).start()
         far_pair(early - 2)
         finish(IJ, e_i, e_j, 1.0)
+        k_copy(turn(0)).start()
         far_pair(early - 1)
 
         core_copy(OK).start()
@@ -308,7 +309,7 @@
         z_copy = remote(z_out, z_in, z_s, z_r, mirror)
         z_copy.start()
 
-        @pl.loop(0, early)
+        @pl.loop(1, early)
         def _(c):
             k_copy(turn(c)).start()
 
@@ -326,9 +327,7 @@
             go_copy(p).wait_send()
         turn_over()
 
-        def inner_result(at):
-            slot = lax.rem(at, 2)
-
+        def inner_result(at, slot):
             def body(cols):
                 stage_i[slot, :, cols] = (
                     product(o_buf[part(at), :], t[OI, :, cols], nn)
@@ -337,31 +336,32 @@
 
             wide_loop(body)
 
-        @pl.loop(0, CHUNKS)
-        def _(c):
-            at = turn(lax.rem(c + early, CHUNKS))
-
-            @pl.when(c < early)
-            def _():
-                k_copy(at).wait_recv()
-
-                @pl.when(c >= 2)
+        @pl.loop(0, early)
+        def _(c):
+            late = turn(c + early)
+            k_copy(late).wait_recv()
+
+            @pl.when(c >= 2)
+            def _():
+                res_copy(turn(c + early - 2)).wait_send()
+
+            outer_result(stage_o, lax.rem(late, 2), x, late)
+            res_copy(late).start()
+            for slot, start in ((0, early), (1, 0)):
+                at = turn(c + start)
+
+                @pl.when(c >= 1)
                 def _():
-                    res_copy(turn(c + early - 2)).wait_send()
-
-                outer_result(stage_o, lax.rem(at, 2), x, at)
-                res_copy(at).start()
-
-            @pl.when(c >= 2)
-            def _():
-                out_copy(turn(lax.rem(c + early - 2, CHUNKS))).wait()
-
-            inner_result(at)
-            out_copy(at).start()
+                    out_copy(turn(c + start - 1), slot).wait()
+
+                inner_result(at, slot)
+                out_copy(at, slot).start()
+
+        out_copy(turn(CHUNKS - 1), 0).wait()
+        out_copy(turn(early - 1), 1).wait()
 
         @pl.loop(CHUNKS - 2, CHUNKS)
         def _(c):
-            out_copy(turn(c - early)).wait()
             res_copy(turn(c)).wait_send()
 
         @pl.loop(0, CHUNKS)
@@ -388,7 +388,7 @@
         pltpu.VMEM((half, width), BF16), pltpu.VMEM((half, width), BF16),
         pltpu.VMEM((4, half, width), F32),
         pltpu.VMEM((4, half, width), BF16), pltpu.VMEM((4, half, width), BF16),
-        pltpu.VMEM((3, 8, 128), F32),
+        pltpu.VMEM((width, 8), F32), pltpu.VMEM((3, 8, 128), F32),
     ]
     scratch += [flags((CHUNKS,))] * 8 + [flags((3, CHUNKS))] * 2 + [flags((3,))] * 2 + [flags] * 2
     scratch += [flags((4,))] * 4 + [flags((5,))] * 4 + [flags] * 2 + [flags((3,))]
@@ -396,7 +396,7 @@
     density = pl.pallas_call(
         four_blocks,
         out_shape=jax.ShapeDtypeStruct((rows, width), BF16),
-        in_specs=[vmem] * 4,
+        in_specs=[vmem] * 3,
         out_specs=pl.BlockSpec(memory_space=pl.ANY),
         scratch_shapes=scratch,
         compiler_params=pltpu.CompilerParams(
@@ -404,8 +404,7 @@
     )(
         three_index.reshape(rows, width),
         jnp.broadcast_to(occupied_energy.astype(F32)[:, None], (8, 128)),
-        virtual_energy[None, :],
-        virtual_energy[:, None],
+        virtual_energy.reshape(1, width),
     )
     return density.reshape(rows, 1, width)
 

time: 347 us -> 351 us (1.012)
  Pallas kernels: 337 us -> 342 us
    pallas_call x1, Pallas kernels: 337 us -> 342 us  [cycle_of_four(): pl.pallas_call(four_blocks, out_shape=jax.ShapeDtypeStruct((rows, width),...]
where the time goes in v3:
time: 351 us; the launch traced here: 350 us
  Pallas kernels  342 us (97%)
  local copies, waits for them, and re-layouts  7.77 us (2%)
    pallas_call x1, Pallas kernels, cycle_of_four(): pl.pallas_call(four_blocks, out_shape=jax.ShapeDtypeStruct((rows, width),...  342 us

profile of v3, /device:TPU:0, one launch (start us, length us, event | category | flops | bytes accessed | tf_op | source)
XLA Modules:
  0.0 350.4 jit_solution(9386237856185359276)
XLA Ops:
  0.7 1.3 reshape.11.e_row
  1.9 0.6 broadcast_in_dim.13.e_own
  2.5 341.9 %shard_map.37 = bf16[4096,768]{1,0:T(8,128)(2,1)} custom-call(bf16[4096,768]{1,0:T(8,128)(2,1)} %bitcast.6, f32[8,128]{1,0:T(8,128)} %broadcast_in_dim.13.e_own, f32[1,768]{1,0:T(1,128)} %reshape.11.e_row), custom_call_target="tpu_custom_call" | custom-call | tf_op jit(solution)/shard_map/pallas_call | solution.py:396
  344.5 5.9 %copy.6 = bf16[4096,1,768]{2,0,1:T(8,128)(2,1)} copy(bf16[4096,1,768]{2,0,1:T(8,128)(2,1)} %bitcast.5) | data formatting | bytes 12582912

commit v4 on v3

--- a/solution.py
+++ b/solution.py
@@ -9,7 +9,7 @@
 
 spin_scale = 1.2
 MESH = pl.DeviceIdType.MESH
-CHUNKS = 16
+CHUNKS = 8
 WIDE = 256
 F32, BF16 = jnp.float32, jnp.bfloat16
 
@@ -65,7 +65,7 @@
     return accumulated.astype(jnp.bfloat16).reshape(aux_rows, occ_rows, slab_size)
 
 
-OI, OJ, IJ, OK, KI = range(5)
+OI, OJ, IJ, OK, KI, FAR = range(6)
 
 
 def four_blocks(x, e_own, e_row, out, o_buf, j_buf, k_buf, stage_o, stage_i, g, t,
@@ -150,7 +150,7 @@
             stage[slot, :, cols] = (
                 product(i_block[part(at), :], t[OI, cols, :], nt)
                 + product(j_buf[part(at), :], t[OJ, cols, :], nt)
-                + product(k_buf[part(at), :], t[OK, cols, :], nt)).astype(BF16)
+                + product(k_buf[part(at), :], t[FAR, cols, :], nt)).astype(BF16)
 
         wide_loop(body)
 
@@ -161,9 +161,13 @@
         wide_loop(body)
 
     def turn_over():
+        @pl.when(z < 2)
+        def _():
+            t[FAR] = t[OK]
+
         @pl.when(z >= 2)
         def _():
-            t[OK] = t[OK].T
+            t[FAR] = t[OK].T
 
     energies = [remote(e_own, e_buf.at[d], e_s.at[d], e_r.at[d], around[d]) for d in range(3)]
     for copy in energies:
@@ -299,7 +303,6 @@
         go_copy(OI).start()
         far_pair(early - 2)
         finish(IJ, e_i, e_j, 1.0)
-        k_copy(turn(0)).start()
         far_pair(early - 1)
 
         core_copy(OK).start()
@@ -309,7 +312,7 @@
         z_copy = remote(z_out, z_in, z_s, z_r, mirror)
         z_copy.start()
 
-        @pl.loop(1, early)
+        @pl.loop(0, early)
         def _(c):
             k_copy(turn(c)).start()
 
@@ -319,15 +322,16 @@
         x_copy(OK).start()
         ki_copy.wait()
         t_copy(KI).start()
-        finish(OK, jnp.where(z == 1, e_o, e_k), jnp.where(z == 1, e_k, e_o), 1.0)
-        go_copy(OK).start()
-        for p in (OJ, OI, IJ, KI, OK):
+        for p in (OJ, OI, IJ, KI):
             t_copy(p).wait()
-        for p in (OJ, OI, OK):
-            go_copy(p).wait_send()
-        turn_over()
-
-        def inner_result(at, slot):
+
+        def inner_result(c):
+            at, slot = turn(c), lax.rem(c, 2)
+
+            @pl.when(c >= 2)
+            def _():
+                out_copy(turn(c - 2), slot).wait()
+
             def body(cols):
                 stage_i[slot, :, cols] = (
                     product(o_buf[part(at), :], t[OI, :, cols], nn)
@@ -335,30 +339,36 @@
                     + product(k_buf[part(at), :], t[KI, :, cols], nn)).astype(BF16)
 
             wide_loop(body)
+            out_copy(at, slot).start()
 
         @pl.loop(0, early)
         def _(c):
-            late = turn(c + early)
-            k_copy(late).wait_recv()
-
-            @pl.when(c >= 2)
-            def _():
-                res_copy(turn(c + early - 2)).wait_send()
-
-            outer_result(stage_o, lax.rem(late, 2), x, late)
-            res_copy(late).start()
-            for slot, start in ((0, early), (1, 0)):
-                at = turn(c + start)
-
-                @pl.when(c >= 1)
-                def _():
-                    out_copy(turn(c + start - 1), slot).wait()
-
-                inner_result(at, slot)
-                out_copy(at, slot).start()
-
-        out_copy(turn(CHUNKS - 1), 0).wait()
-        out_copy(turn(early - 1), 1).wait()
+            inner_result(c)
+
+        finish(OK, jnp.where(z == 1, e_o, e_k), jnp.where(z == 1, e_k, e_o), 1.0)
+        go_copy(OK).start()
+        t_copy(OK).wait()
+        turn_over()
+
+        @pl.loop(early, CHUNKS)
+        def _(c):
+            at = turn(c)
+            k_copy(at).wait_recv()
+
+            @pl.when(c >= early + 2)
+            def _():
+                res_copy(turn(c - 2)).wait_send()
+
+            outer_result(stage_o, lax.rem(at, 2), x, at)
+            res_copy(at).start()
+            inner_result(c)
+
+        for p in (OJ, OI, OK):
+            go_copy(p).wait_send()
+
+        @pl.loop(CHUNKS - 2, CHUNKS)
+        def _(c):
+            out_copy(turn(c), lax.rem(c, 2)).wait()
 
         @pl.loop(CHUNKS - 2, CHUNKS)
         def _(c):
@@ -384,7 +394,7 @@
         pltpu.VMEM((rows, width), BF16), pltpu.VMEM((rows, width), BF16),
         pltpu.VMEM((rows, width), BF16),
         pltpu.VMEM((2, size, width), BF16), pltpu.VMEM((2, size, width), BF16),
-        pltpu.VMEM((4, width, width), F32), pltpu.VMEM((5, width, width), BF16),
+        pltpu.VMEM((4, width, width), F32), pltpu.VMEM((6, width, width), BF16),
         pltpu.VMEM((half, width), BF16), pltpu.VMEM((half, width), BF16),
         pltpu.VMEM((4, half, width), F32),
         pltpu.VMEM((4, half, width), BF16), pltpu.VMEM((4, half, width), BF16),

time: 351 us -> 345 us (0.983)
  Pallas kernels: 342 us -> 336 us
    pallas_call x1, Pallas kernels: 342 us -> 336 us  [cycle_of_four(): pl.pallas_call(four_blocks, out_shape=jax.ShapeDtypeStruct((rows, width),...]
where the time goes in v4:
time: 345 us
  Pallas kernels  336 us (97%)
  local copies, waits for them, and re-layouts  7.77 us (2%)
    pallas_call x1, Pallas kernels, cycle_of_four(): pl.pallas_call(four_blocks, out_shape=jax.ShapeDtypeStruct((rows, width),...  336 us

profile of v4, /device:TPU:0, one launch (start us, length us, event | category | flops | bytes accessed | tf_op | source)
XLA Modules:
  0.0 344.9 jit_solution(3258264360453332952)
XLA Ops:
  0.7 1.3 reshape.11.e_row
  1.9 0.6 broadcast_in_dim.13.e_own
  2.5 336.5 %shard_map.37 = bf16[4096,768]{1,0:T(8,128)(2,1)} custom-call(bf16[4096,768]{1,0:T(8,128)(2,1)} %bitcast.6, f32[8,128]{1,0:T(8,128)} %broadcast_in_dim.13.e_own, f32[1,768]{1,0:T(1,128)} %reshape.11.e_row), custom_call_target="tpu_custom_call" | custom-call | tf_op jit(solution)/shard_map/pallas_call | solution.py:406
  339.0 5.9 %copy.6 = bf16[4096,1,768]{2,0,1:T(8,128)(2,1)} copy(bf16[4096,1,768]{2,0,1:T(8,128)(2,1)} %bitcast.5) | data formatting | bytes 12582912

commit v5 on v4

--- a/solution.py
+++ b/solution.py
@@ -155,10 +155,7 @@
         wide_loop(body)
 
     def gram(pair, left, right, at):
-        def body(cols):
-            g[pair, :, cols] += product(left[part(at), :], right[part(at), cols], tn)
-
-        wide_loop(body)
+        g[pair] += product(left[part(at), :], right[part(at), :], tn)
 
     def turn_over():
         @pl.when(z < 2)

time: 345 us -> 345 us (level)
  no operation moved by 1% of the time
where the time goes in v5:
time: 345 us
  Pallas kernels  336 us (97%)
  local copies, waits for them, and re-layouts  7.77 us (2%)
    pallas_call x1, Pallas kernels, cycle_of_four(): pl.pallas_call(four_blocks, out_shape=jax.ShapeDtypeStruct((rows, width),...  336 us

profile of v5, /device:TPU:0, one launch (start us, length us, event | category | flops | bytes accessed | tf_op | source)
XLA Modules:
  0.0 344.9 jit_solution(6313958809486902003)
XLA Ops:
  0.7 1.3 reshape.11.e_row
  1.9 0.6 broadcast_in_dim.13.e_own
  2.5 336.5 %shard_map.37 = bf16[4096,768]{1,0:T(8,128)(2,1)} custom-call(bf16[4096,768]{1,0:T(8,128)(2,1)} %bitcast.6, f32[8,128]{1,0:T(8,128)} %broadcast_in_dim.13.e_own, f32[1,768]{1,0:T(1,128)} %reshape.11.e_row), custom_call_target="tpu_custom_call" | custom-call | tf_op jit(solution)/shard_map/pallas_call | solution.py:403
  339.0 5.9 %copy.6 = bf16[4096,1,768]{2,0,1:T(8,128)(2,1)} copy(bf16[4096,1,768]{2,0,1:T(8,128)(2,1)} %bitcast.5) | data formatting | bytes 12582912
